TPU v7x, 128 devices: a whole 4x4x4 slice. The times are simulated.
128 devices in a mesh: det: 16 (over z_lo, x, core), strip: 8 (over y, z_hi).
Axes of the slice: x: 4, y: 4, z: 4 (z_hi: 2, z_lo: 2; z = z_hi * 2 + z_lo), core: 2. Of those that a mesh axis runs over, the one named last changes fastest.
Arguments:
- science: float32 [16, 256, 4096], P('det', 'strip'), may hold values from -17 to 17
- template: float32 [16, 256, 4096], P(None, 'strip', 'det'), may hold values from -8 to 8
- row_taps: float32 [12, 21], replicated, may hold values from -1.25 to 1.25
- col_taps: float32 [12, 21], replicated, may hold values from -1.25 to 1.25
- stamp_rows: int32 [16, 32], P('det'), may hold values from 17 to 238
- stamp_cols: int32 [16, 32], P('det'), may hold values from 17 to 4078
Outputs:
- difference: float32 [16, 256, 4096], P('det', 'strip')
- kernel_coeffs: float32 [16, 37], P('det')
All inputs are finite; a program needn't handle non-finite values.
Results may differ from a plain program's by a relative error of at most 0.0003.
Values sent between devices are 32-bit elements; how exact they have to be, the bound alone decides.
A program may use at most 128 MiB of HBM per device.

v0:
```python
import jax
import jax.numpy as jnp
from jax import lax
from jax.sharding import PartitionSpec as P

NB = 12
KS = 21
HS = 17
KH = 10
NU = 37
RIDGE_WEIGHT = 1.0
HIGHEST_MODE = lax.Precision.HIGHEST
LANE_WIDTH = 128


def padded_2(block, sides, width):
    for axis, dim in sides:
        count = lax.axis_size(axis)
        forward = [(i, i + 1) for i in range(count - 1)]
        backward = [(target, source) for source, target in forward]
        low = lax.ppermute(
            lax.slice_in_dim(block, block.shape[dim] - width, None, axis=dim), axis, forward
        )
        high = lax.ppermute(lax.slice_in_dim(block, 0, width, axis=dim), axis, backward)
        block = jnp.concatenate([low, block, high], axis=dim)
    return block


def column_tables(col_taps):
    offset = jnp.arange(2 * LANE_WIDTH)[:, None] - jnp.arange(LANE_WIDTH)[None, :]
    onehot = (offset[None] == jnp.arange(KS)[:, None, None]).astype(jnp.float32)
    whole = jnp.einsum("bv,vij->bij", col_taps, onehot, precision=HIGHEST_MODE)
    return (whole[:, :LANE_WIDTH, :], whole[:, LANE_WIDTH:, :])


def row_table(row_taps, row_count):
    offset = jnp.arange(row_count + 2 * KH)[None, :] - jnp.arange(row_count)[:, None]
    onehot = (offset[None] == jnp.arange(KS)[:, None, None]).astype(jnp.float32)
    return jnp.einsum("bv,vyk->byk", row_taps, onehot, precision=HIGHEST_MODE)


def correlate(framed, main_tab, next_tab, row_tab):
    depth, col_count = framed.shape
    col_blocks = col_count // LANE_WIDTH
    padded = jnp.pad(framed, ((0, 0), (KH, LANE_WIDTH - KH)))
    central = padded[:, :col_count].reshape(depth, col_blocks, LANE_WIDTH)
    following = padded[:, LANE_WIDTH : col_count + LANE_WIDTH].reshape(
        depth, col_blocks, LANE_WIDTH
    )
    across = jnp.einsum("rki,bij->brkj", central, main_tab, precision=HIGHEST_MODE)
    across = across + jnp.einsum("rki,bij->brkj", following, next_tab, precision=HIGHEST_MODE)
    across = across.reshape(NB, depth, col_count)
    return jnp.einsum("byk,bkc->byc", row_tab, across, precision=HIGHEST_MODE)


def apply_model(responses, coeffs, y_coord, x_coord):
    base_part = jnp.tensordot(coeffs[:NB], responses, axes=1, precision=HIGHEST_MODE)
    x_part = jnp.tensordot(coeffs[NB : 2 * NB], responses, axes=1, precision=HIGHEST_MODE)
    y_part = jnp.tensordot(coeffs[2 * NB : 3 * NB], responses, axes=1, precision=HIGHEST_MODE)
    return base_part + x_coord * x_part + y_coord * y_part + coeffs[NU - 1]


def local(science, template, row_taps, col_taps, stamp_rows, stamp_cols):
    det_count, row_count, col_count = science.shape
    moved = lax.all_to_all(template, "det", split_axis=0, concat_axis=2, tiled=True)
    framed = padded_2(moved, (("strip", 1),), KH)
    total_rows = row_count * lax.axis_size("strip")
    first_global = lax.axis_index("strip") * row_count
    global_rows = first_global + jnp.arange(row_count, dtype=jnp.int32)
    y_coord = (2.0 * global_rows.astype(jnp.float32) / total_rows - 1.0)[:, None]
    col_index = jnp.arange(col_count, dtype=jnp.int32)
    x_coord = (2.0 * col_index.astype(jnp.float32) / col_count - 1.0)[None, :]
    main_tab, next_tab = column_tables(col_taps)
    row_tab = row_table(row_taps, row_count)
    y_flat = jnp.broadcast_to(y_coord, (row_count, col_count)).reshape(1, -1)
    x_flat = jnp.broadcast_to(x_coord, (row_count, col_count)).reshape(1, -1)
    unity = jnp.ones((1, row_count * col_count), jnp.float32)
    responses = correlate(framed[0], main_tab, next_tab, row_tab)
    observed = science[0]
    row_hits = (jnp.abs(global_rows[:, None] - stamp_rows[0][None, :]) <= HS).astype(jnp.float32)
    col_hits = (jnp.abs(stamp_cols[0][:, None] - col_index[None, :]) <= HS).astype(jnp.float32)
    weight = jnp.dot(
        row_hits, col_hits, precision=HIGHEST_MODE, preferred_element_type=jnp.float32
    ).reshape(1, -1)
    flat = responses.reshape(NB, -1)
    feats = jnp.concatenate([flat, flat * x_flat, flat * y_flat, unity], axis=0)
    weighted = feats * weight
    normal = jnp.einsum("ip,jp->ij", weighted, feats, precision=HIGHEST_MODE)
    target = jnp.einsum("ip,p->i", weighted, observed.reshape(-1), precision=HIGHEST_MODE)
    normal, target = lax.psum((normal, target), "strip")
    normal = normal + RIDGE_WEIGHT * jnp.eye(NU, dtype=jnp.float32)
    factor = jnp.linalg.cholesky(normal)
    coeffs = jax.scipy.linalg.cho_solve((factor, True), target)
    differences = [observed - apply_model(responses, coeffs, y_coord, x_coord)]
    solutions = [coeffs]
    return (jnp.stack(differences), jnp.stack(solutions))


def solution(mesh):
    return jax.shard_map(
        local,
        mesh=mesh,
        in_specs=(
            P("det", "strip", None),
            P(None, "strip", "det"),
            P(),
            P(),
            P("det", None),
            P("det", None),
        ),
        out_specs=(P("det", "strip", None), P("det", None)),
        check_vma=False,
    )
```

profile of v0, /device:TPU:0, one launch (start us, length us, event | category | flops | bytes accessed | tf_op | source)
XLA Modules:
  0.0 230.5 jit_solution(16646424460032151319)
XLA Ops:
  0.7 6.1 %all-to-all-start = ((f32[16,32,256]{2,1,0:T(8,128)}), f32[16,32,256]{2,1,0:T(8,128)}, u32[]{:S(2)}, u32[]{:S(2)}) async-start(f32[16,32,256]{2,1,0:T(8,128)} %param.7), calls=%async_computation | async-start | bytes 1048576 | tf_op jit(solution)/shard_map/all_to_all | solution.py:65
  7.2 1.0 convolution_bitcast_fusion
  8.2 0.9 copy.36
  9.1 2.4 %copy.37 = f32[1,1,32,4096]{3,1,2,0:T(1,128)} copy(f32[1,1,32,4096]{3,2,1,0:T(8,128)} %bitcast.123) | data formatting | bytes 1048576
  11.4 1.4 fusion.15
  13.1 4.5 %all-to-all-done = f32[16,32,256]{2,1,0:T(8,128)} async-done(((f32[16,32,256]{2,1,0:T(8,128)}), f32[16,32,256]{2,1,0:T(8,128)}, u32[]{:S(2)}, u32[]{:S(2)}) %all-to-all-start) | async-done | bytes 524320 | tf_op jit(solution)/shard_map/all_to_all | solution.py:65
  17.6 1.1 copy.30
  18.7 5.5 %collective-permute-start = (f32[1,10,4096]{2,1,0:T(8,128)S(1)}, f32[1,10,4096]{2,1,0:T(8,128)S(1)}, u32[]{:S(2)}, u32[]{:S(2)}) collective-permute-start(f32[1,10,4096]{2,1,0:T(8,128)S(1)} %get-tuple-element.10), channel_id=1, source_target_pairs={{0,1},{1,2},{2,3},{3,4},{4,5},{5,6},{6,7},{8,9},{9,10},{10,11},{11... | collective-permute-start | bytes 491528 | tf_op jit(solution)/shard_map/ppermute | solution.py:21
  24.3 1.5 collective-permute-start.1
  26.0 8.6 %collective-permute-done = f32[1,10,4096]{2,1,0:T(8,128)S(1)} collective-permute-done((f32[1,10,4096]{2,1,0:T(8,128)S(1)}, f32[1,10,4096]{2,1,0:T(8,128)S(1)}, u32[]{:S(2)}, u32[]{:S(2)}) %collective-permute-start) | collective-permute-done | bytes 163872 | tf_op jit(solution)/shard_map/ppermute | solution.py:21
  35.8 9.2 %fusion.21 = f32[12,128,52,32]{1,2,3,0:T(8,128)S(1)} fusion(f32[52,32,128]{2,1,0:T(8,128)S(1)} %slice.63, f32[12,128,128,1]{2,0,1,3:T(8,128)S(1)} %get-tuple-element.7), kind=kOutput, calls=%fused_computation.29 | convolution fusion | flops 3925868544 | bytes 11862016 | tf_op jit(solution)/shard_map/rki,bij->brkj/dot_general | solution.py:50
  45.0 10.5 %add_bitcast_fusion = f32[12,52,32,128]{3,1,2,0:T(8,128)S(1)} fusion(f32[12,128,52,32]{1,2,3,0:T(8,128)S(1)} %fusion.21, f32[52,32,128]{2,1,0:T(8,128)S(1)} %slice.64, f32[12,128,128,1]{2,0,1,3:T(8,128)S(1)} %get-tuple-element.6), kind=kOutput, calls=%fused_computation.5 | convolution fusion | flops 3928424448 | bytes 22085632 | tf_op jit(solution)/shard_map/rki,bij->brkj/dot_general | solution.py:51
  55.5 5.5 %copy.16 = f32[12,52,32,128]{3,2,1,0:T(8,128)} copy(f32[12,52,32,128]{3,1,2,0:T(8,128)S(1)} %add_bitcast_fusion) | data formatting | bytes 20447232 | tf_op jit(solution)/shard_map/add | solution.py:51
  61.0 10.2 %reshape.85 = f32[12,52,4096]{2,1,0:T(8,128)} reshape(f32[12,52,32,128]{3,2,1,0:T(8,128)} %copy.16) | data formatting | bytes 20447232 | tf_op jit(solution)/shard_map/reshape | solution.py:52
  71.2 9.3 %fusion.36 = f32[12,32,4096]{2,1,0:T(8,128)S(1)} fusion(f32[12,52,4096]{2,1,0:T(8,128)} %reshape.85, f32[32,52,12]{1,2,0:T(8,128)S(1)} %fusion.32), kind=kOutput, calls=%fused_computation.52 | convolution fusion | flops 981467136 | bytes 16594944 | tf_op jit(solution)/shard_map/byk,bkc->byc/dot_general | solution.py:53
  80.5 2.7 %copy-done.2 = f32[12,32,4096]{2,1,0:T(8,128)} copy-done((f32[12,32,4096]{2,1,0:T(8,128)}, f32[12,32,4096]{2,1,0:T(8,128)S(1)}, u32[]{:S(2)}) %copy-start.2) | copy-done | bytes 6291480
  83.2 0.9 pad.12
  84.1 4.9 %copy.33 = f32[2,8,32,4096]{3,1,2,0:T(8,128)S(1)} copy(f32[2,8,32,4096]{3,2,1,0:T(8,128)S(1)} %bitcast.116) | data formatting | bytes 16777216
  89.0 6.6 %broadcast_multiply_fusion.1 = (f32[12,131072]{1,0:T(8,128)}, f32[12,131072]{1,0:T(8,128)}) fusion(f32[12,131072]{1,0:T(8,128)S(1)} %bitcast.113, f32[131072]{0:T(1024)S(1)} %bitcast.125, f32[131072]{0:T(1024)S(1)} %bitcast.124), kind=kLoop, calls=%fused_computation.17 | loop fusion | flops 3145728 | bytes 19922944 | tf_op jit(solution)/shard_map/mul | solution.py:86
  95.7 1.6 copy-done.3
  97.3 26.7 %fusion.2 = f32[37,37]{1,0:T(8,128)S(1)} fusion(f32[12,131072]{1,0:T(8,128)} %get-tuple-element.5, f32[12,131072]{1,0:T(8,128)} %get-tuple-element.4, f32[12,131072]{1,0:T(8,128)} %bitcast.114, f32[37]{0:T(128)S(1)} %pad.8.clone, f32[131072]{0:T(1024)S(1)} %bitcast.126), kind=kOutput, calls=%fused_computation.2 | convolution fusion | flops 2187198464 | bytes 19404280 | tf_op jit(solution)/shard_map/ip,jp->ij/dot_general | solution.py:88
  124.0 21.7 %fusion.17 = f32[37]{0:T(128)S(1)} fusion(f32[131072,1]{0,1:T(1,128)S(1)} %bitcast.128, f32[12,131072]{1,0:T(8,128)} %get-tuple-element.5, f32[12,131072]{1,0:T(8,128)} %get-tuple-element.4, f32[12,131072]{1,0:T(8,128)} %bitcast.115, f32[37]{0:T(128)S(1)} %pad.8.clone, f32[131072]{0:T(1024)S(1)} %bitcast.127), kind=kOutput, calls=%fused_computation.23 | convolution fusion | flops 77594624 | bytes 19923240 | tf_op jit(solution)/shard_map/ip,p->i/dot_general | solution.py:89
  145.7 41.4 %all-reduce.1 = (f32[37,37]{1,0:T(8,128)S(1)}, f32[37]{0:T(128)S(1)}) all-reduce(f32[37,37]{1,0:T(8,128)S(1)} %fusion.2, f32[37]{0:T(128)S(1)} %fusion.17), channel_id=1, replica_groups=mesh['det'=16,'strip'=8] {'strip'}, use_global_device_ids=true, to_apply=%region_0.1 | all-reduce | flops 1406 | bytes 11248 | tf_op jit(solution)/shard_map/psum | solution.py:90
  187.2 3.4 %cholesky.17 = f32[37,37]{1,0:T(8,128)S(1)} custom-call(f32[37,37]{1,0:T(8,128)S(1)} %fusion.43), custom_call_target="Cholesky" | custom-call | tf_op jit(solution)/shard_map/jit(cholesky)/cholesky | solution.py:92
  190.6 0.6 compare_reduce_fusion
  191.2 0.7 fusion.39
  191.9 2.8 %custom-call.10 = f32[1,37,37]{1,2,0:T(8,128)S(1)} custom-call(f32[1,37,37]{2,1,0:T(8,128)S(1)} %fusion.39), custom_call_target="InvertDiagBlocksLowerTriangular" | custom-call | tf_op jit(solution)/shard_map/jit(_cho_solve)/triangular_solve | solution.py:93
  195.0 11.3 %fusion.12 = f32[1,32,4096]{2,0,1:T(1,128)S(1)} fusion(f32[12,32,4096]{2,1,0:T(8,128)} %copy-done.2, f32[37]{0:T(128)S(1)} %bitcast.129), kind=kOutput, calls=%fused_computation.14 | convolution fusion | flops 18874368 | bytes 6815892 | tf_op jit(solution)/shard_map/dot_general | solution.py:57
  206.4 11.4 %fusion.10 = f32[1,32,4096]{2,0,1:T(1,128)S(1)} fusion(f32[12,32,4096]{2,1,0:T(8,128)} %copy-done.2, f32[37]{0:T(128)S(1)} %bitcast.130), kind=kOutput, calls=%fused_computation.12 | convolution fusion | flops 18874368 | bytes 6815892 | tf_op jit(solution)/shard_map/dot_general | solution.py:58
  217.8 9.3 %fusion.8 = f32[1,32,4096]{2,0,1:T(1,128)S(1)} fusion(f32[12,32,4096]{2,1,0:T(8,128)S(1)} %bitcast.112, f32[37]{0:T(128)S(1)} %bitcast.131), kind=kOutput, calls=%fused_computation.10 | convolution fusion | flops 18874368 | bytes 6815892 | tf_op jit(solution)/shard_map/dot_general | solution.py:59
  227.1 0.6 slice.58
  227.7 2.5 %fusion.30 = f32[1,32,4096]{2,1,0:T(8,128)} fusion(f32[1,32,4096]{2,1,0:T(8,128)S(1)} %copy-done.4, f32[1,32,4096]{2,0,1:T(1,128)S(1)} %fusion.8, f32[1,32,4096]{2,0,1:T(1,128)S(1)} %fusion.10, f32[1,32,4096]{2,0,1:T(1,128)S(1)} %fusion.12, f32[]{:T(128)} %bitcast.29, f32[32]{0:T(128)S(1)} %multiply_add_fusion.1, f32[4096]{0:T(1024)S(1)} %multiply_add_fusion), kind=kLoop, calls=%fused_computation.41 | loop fusion | flops 786432 | bytes 2637956 | tf_op jit(solution)/shard_map/stack | solution.py:96
  (48 shorter events, 2.5 us)
Async XLA Ops:
  0.6 10.8 %copy-start = (f32[12,21]{1,0:T(8,128)S(1)}, f32[12,21]{1,0:T(8,128)}, u32[]{:S(2)}) copy-start(f32[12,21]{1,0:T(8,128)} %param.9) | copy-start | bytes 3028
  0.6 25.1 %copy-start.8 = (f32[12,21]{1,0:T(8,128)S(1)}, f32[12,21]{1,0:T(8,128)}, u32[]{:S(2)}) copy-start(f32[12,21]{1,0:T(8,128)} %param.8) | copy-start | bytes 3028
  0.7 17.0 %all-to-all-start = ((f32[16,32,256]{2,1,0:T(8,128)}), f32[16,32,256]{2,1,0:T(8,128)}, u32[]{:S(2)}, u32[]{:S(2)}) async-start(f32[16,32,256]{2,1,0:T(8,128)} %param.7), calls=%async_computation | async-start | bytes 1048576 | tf_op jit(solution)/shard_map/all_to_all | solution.py:65
  18.7 15.9 %collective-permute-start = (f32[1,10,4096]{2,1,0:T(8,128)S(1)}, f32[1,10,4096]{2,1,0:T(8,128)S(1)}, u32[]{:S(2)}, u32[]{:S(2)}) collective-permute-start(f32[1,10,4096]{2,1,0:T(8,128)S(1)} %get-tuple-element.10), channel_id=1, source_target_pairs={{0,1},{1,2},{2,3},{3,4},{4,5},{5,6},{6,7},{8,9},{9,10},{10,11},{11... | collective-permute-start | bytes 491528 | tf_op jit(solution)/shard_map/ppermute | solution.py:21
  24.3 10.4 %collective-permute-start.1 = (f32[1,10,4096]{2,1,0:T(8,128)S(1)}, f32[1,10,4096]{2,1,0:T(8,128)S(1)}, u32[]{:S(2)}, u32[]{:S(2)}) collective-permute-start(f32[1,10,4096]{2,1,0:T(8,128)S(1)} %get-tuple-element.11), channel_id=1, source_target_pairs={{1,0},{2,1},{3,2},{4,3},{5,4},{6,5},{7,6},{9,8},{10,9},{11,10},{12... | collective-permute-start | bytes 491528 | tf_op jit(solution)/shard_map/ppermute | solution.py:24
  80.5 2.7 %copy-start.2 = (f32[12,32,4096]{2,1,0:T(8,128)}, f32[12,32,4096]{2,1,0:T(8,128)S(1)}, u32[]{:S(2)}) copy-start(f32[12,32,4096]{2,1,0:T(8,128)S(1)} %fusion.36) | copy-start | bytes 18874372
  89.0 8.3 %copy-start.3 = (f32[2,8,32,4096]{3,1,2,0:T(8,128)}, f32[2,8,32,4096]{3,1,2,0:T(8,128)S(1)}, u32[]{:S(2)}) copy-start(f32[2,8,32,4096]{3,1,2,0:T(8,128)S(1)} %copy.33) | copy-start | bytes 25165828
  89.0 8.3 %copy-start.5 = (f32[4,32,8,128]{3,1,2,0:T(8,128)S(1)}, f32[4,32,8,128]{3,1,2,0:T(8,128)}, u32[]{:S(2)}) copy-start(f32[4,32,8,128]{3,1,2,0:T(8,128)} %copy.36) | copy-start | bytes 1572868
  97.3 26.7 %copy-start.6 = (f32[1,1,32,4096]{3,1,2,0:T(1,128)S(1)}, f32[1,1,32,4096]{3,1,2,0:T(1,128)}, u32[]{:S(2)}) copy-start(f32[1,1,32,4096]{3,1,2,0:T(1,128)} %copy.37) | copy-start | bytes 1572868
  195.0 32.1 %copy-start.7 = (f32[1,37]{1,0:T(1,128)}, f32[1,37]{1,0:T(1,128)S(1)}, u32[]{:S(2)}) copy-start(f32[1,37]{1,0:T(1,128)S(1)} %fusion.40) | copy-start | bytes 448
  195.0 22.8 %slice-start = ((s8[6291456]{0:T(1024)(128)(4,1)}), s8[4194304]{0:T(1024)(128)(4,1)S(1)}, s32[]{:S(2)}) async-start(s8[6291456]{0:T(1024)(128)(4,1)} %bitcast.111), calls=%async_computation.1 | async-start | bytes 8388608
  195.0 35.2 %copy-start.1 = (f32[12,21]{1,0:T(8,128)S(1)}, f32[12,21]{1,0:T(8,128)}, u32[]{:S(2)}) copy-start(f32[12,21]{1,0:T(8,128)} %param.9) | copy-start | bytes 3028
  206.4 11.4 %slice-start.1 = ((s8[6291456]{0:T(1024)(128)(4,1)}), s8[2097152]{0:T(1024)(128)(4,1)S(1)}, s32[]{:S(2)}) async-start(s8[6291456]{0:T(1024)(128)(4,1)} %bitcast.111), calls=%async_computation.2 | async-start | bytes 4194304
  206.4 21.3 %copy-start.4 = (f32[1,32,4096]{2,1,0:T(8,128)S(1)}, f32[1,32,4096]{2,1,0:T(8,128)}, u32[]{:S(2)}) copy-start(f32[1,32,4096]{2,1,0:T(8,128)} %param.6) | copy-start | bytes 1572868
where the time goes:
time: 234 us; the launch traced here: 230 us
  matrix products  112 us (48%)
  blocking collectives  41.4 us (18%)
  local copies, waits for them, and re-layouts  32.4 us (14%)
  other arithmetic  16.9 us (7%)
  waiting for transfers between devices  13.1 us (6%)
  starting transfers between devices  13 us (6%)
    psum x1, blocking collectives, local(): normal, target = lax.psum((normal, target), 'strip')  41.4 us
    dot_general x1, matrix products, local(): normal = jnp.einsum('ip,jp->ij', weighted, feats, precision=HIGHEST_MODE)  26.7 us
    dot_general x1, matrix products, local(): jnp.einsum('ip,p->i', weighted, observed.reshape(-1), precision=HIGHEST_M...  21.7 us
    unnamed x32, local copies, waits for them, and re-layouts  14 us
    dot_general x1, matrix products, apply_model(): jnp.tensordot(coeffs[NB:2 * NB], responses, axes=1, precision=HIGHEST_MODE)  11.4 us
    dot_general x1, matrix products, apply_model(): jnp.tensordot(coeffs[:NB], responses, axes=1, precision=HIGHEST_MODE)  11.3 us
    dot_general x1, matrix products, correlate(): jnp.einsum('rki,bij->brkj', following, next_tab, precision=HIGHEST_MODE)  10.5 us
    reshape x1, local copies, waits for them, and re-layouts, correlate(): across = across.reshape(NB, depth, col_count)  10.2 us
  transfers between devices with their start and end apart: 3, of which 2 were waited for; matrix products, arithmetic and copies ran while one was open for 3% of the time, Pallas kernels for 0%

commit v1 on v0

--- a/solution.py
+++ b/solution.py
@@ -62,7 +62,11 @@
 
 def local(science, template, row_taps, col_taps, stamp_rows, stamp_cols):
     det_count, row_count, col_count = science.shape
-    moved = lax.all_to_all(template, "det", split_axis=0, concat_axis=2, tiled=True)
+    draw_loops_all = lambda join_dim, raw, d_out: jnp.concatenate(
+        lax.all_to_all(jnp.stack(jnp.split(raw, lax.axis_size("det"), axis=join_dim)), "det", 0, 0),
+        d_out,
+    )
+    moved = draw_loops_all(0, template, 2)
     framed = padded_2(moved, (("strip", 1),), KH)
     total_rows = row_count * lax.axis_size("strip")
     first_global = lax.axis_index("strip") * row_count

time: 234 us -> 257 us (1.098)
  local copies, waits for them, and re-layouts: 32.4 us -> 54.4 us
    unnamed x32 -> x47, local copies, waits for them, and re-layouts: 14 us -> 34.7 us
where the time goes in v1:
time: 257 us; the launch traced here: 252 us
  matrix products  112 us (44%)
  local copies, waits for them, and re-layouts  54.4 us (21%)
  blocking collectives  41.4 us (16%)
  other arithmetic  16.9 us (7%)
  waiting for transfers between devices  13.1 us (5%)
  starting transfers between devices  12.9 us (5%)
    psum x1, blocking collectives, local(): normal, target = lax.psum((normal, target), 'strip')  41.4 us
    unnamed x47, local copies, waits for them, and re-layouts  34.7 us
    dot_general x1, matrix products, local(): normal = jnp.einsum('ip,jp->ij', weighted, feats, precision=HIGHEST_MODE)  26.7 us
    dot_general x1, matrix products, local(): jnp.einsum('ip,p->i', weighted, observed.reshape(-1), precision=HIGHEST_M...  21.7 us
    dot_general x1, matrix products, apply_model(): jnp.tensordot(coeffs[NB:2 * NB], responses, axes=1, precision=HIGHEST_MODE)  11.4 us
    dot_general x1, matrix products, apply_model(): jnp.tensordot(coeffs[:NB], responses, axes=1, precision=HIGHEST_MODE)  11.3 us
    dot_general x1, matrix products, correlate(): jnp.einsum('rki,bij->brkj', following, next_tab, precision=HIGHEST_MODE)  10.5 us
    reshape x1, local copies, waits for them, and re-layouts, correlate(): across = across.reshape(NB, depth, col_count)  10.2 us
  transfers between devices with their start and end apart: 3, of which 2 were waited for; matrix products, arithmetic and copies ran while one was open for 3% of the time, Pallas kernels for 0%

profile of v1, /device:TPU:0, one launch (start us, length us, event | category | flops | bytes accessed | tf_op | source)
XLA Modules:
  0.0 252.3 jit_solution(15528039854793234216)
XLA Ops:
  0.7 1.4 constant_dynamic-update-slice_fusion.15
  2.0 1.4 constant_dynamic-update-slice_fusion.14
  3.4 1.4 constant_dynamic-update-slice_fusion.13
  7.5 1.4 constant_dynamic-update-slice_fusion.10
  10.3 1.4 constant_dynamic-update-slice_fusion.8
  13.0 1.4 constant_dynamic-update-slice_fusion.6
  15.8 1.4 constant_dynamic-update-slice_fusion.4
  22.7 5.9 %all-to-all-start = ((f32[16,1,32,256]{3,2,1,0:T(8,128)}), f32[16,1,32,256]{3,2,1,0:T(8,128)}, u32[]{:S(2)}, u32[]{:S(2)}) async-start(f32[16,1,32,256]{3,2,1,0:T(8,128)} %constant_dynamic-update-slice_fusion), calls=%async_computation | async-start | bytes 1048576 | tf_op jit(solution)/shard_map/all_to_all | solution.py:66
  30.9 2.4 copy.37
  33.3 1.4 fusion.15
  35.0 4.5 %all-to-all-done = f32[16,1,32,256]{3,2,1,0:T(8,128)} async-done(((f32[16,1,32,256]{3,2,1,0:T(8,128)}), f32[16,1,32,256]{3,2,1,0:T(8,128)}, u32[]{:S(2)}, u32[]{:S(2)}) %all-to-all-start) | async-done | bytes 524320 | tf_op jit(solution)/shard_map/all_to_all | solution.py:66
  40.6 5.5 %collective-permute-start = (f32[1,10,4096]{2,1,0:T(8,128)S(1)}, f32[1,10,4096]{2,1,0:T(8,128)S(1)}, u32[]{:S(2)}, u32[]{:S(2)}) collective-permute-start(f32[1,10,4096]{2,1,0:T(8,128)S(1)} %get-tuple-element.10), channel_id=1, source_target_pairs={{0,1},{1,2},{2,3},{3,4},{4,5},{5,6},{6,7},{8,9},{9,10},{10,11},{11... | collective-permute-start | bytes 491528 | tf_op jit(solution)/shard_map/ppermute | solution.py:21
  46.1 1.5 collective-permute-start.1
  47.9 8.6 %collective-permute-done = f32[1,10,4096]{2,1,0:T(8,128)S(1)} collective-permute-done((f32[1,10,4096]{2,1,0:T(8,128)S(1)}, f32[1,10,4096]{2,1,0:T(8,128)S(1)}, u32[]{:S(2)}, u32[]{:S(2)}) %collective-permute-start) | collective-permute-done | bytes 163872 | tf_op jit(solution)/shard_map/ppermute | solution.py:21
  57.6 9.2 %fusion.21 = f32[12,128,52,32]{1,2,3,0:T(8,128)S(1)} fusion(f32[52,32,128]{2,1,0:T(8,128)S(1)} %slice.63, f32[12,128,128,1]{2,0,1,3:T(8,128)S(1)} %get-tuple-element.7), kind=kOutput, calls=%fused_computation.29 | convolution fusion | flops 3925868544 | bytes 11862016 | tf_op jit(solution)/shard_map/rki,bij->brkj/dot_general | solution.py:50
  66.8 10.5 %add_bitcast_fusion = f32[12,52,32,128]{3,1,2,0:T(8,128)S(1)} fusion(f32[12,128,52,32]{1,2,3,0:T(8,128)S(1)} %fusion.21, f32[52,32,128]{2,1,0:T(8,128)S(1)} %slice.64, f32[12,128,128,1]{2,0,1,3:T(8,128)S(1)} %get-tuple-element.6), kind=kOutput, calls=%fused_computation.5 | convolution fusion | flops 3928424448 | bytes 22085632 | tf_op jit(solution)/shard_map/rki,bij->brkj/dot_general | solution.py:51
  77.4 5.5 %copy.16 = f32[12,52,32,128]{3,2,1,0:T(8,128)} copy(f32[12,52,32,128]{3,1,2,0:T(8,128)S(1)} %add_bitcast_fusion) | data formatting | bytes 20447232 | tf_op jit(solution)/shard_map/add | solution.py:51
  82.9 10.2 %reshape.93 = f32[12,52,4096]{2,1,0:T(8,128)} reshape(f32[12,52,32,128]{3,2,1,0:T(8,128)} %copy.16) | data formatting | bytes 20447232 | tf_op jit(solution)/shard_map/reshape | solution.py:52
  93.1 9.3 %fusion.36 = f32[12,32,4096]{2,1,0:T(8,128)S(1)} fusion(f32[12,52,4096]{2,1,0:T(8,128)} %reshape.93, f32[32,52,12]{1,2,0:T(8,128)S(1)} %fusion.32), kind=kOutput, calls=%fused_computation.52 | convolution fusion | flops 981467136 | bytes 16594944 | tf_op jit(solution)/shard_map/byk,bkc->byc/dot_general | solution.py:53
  102.4 2.7 %copy-done.2 = f32[12,32,4096]{2,1,0:T(8,128)} copy-done((f32[12,32,4096]{2,1,0:T(8,128)}, f32[12,32,4096]{2,1,0:T(8,128)S(1)}, u32[]{:S(2)}) %copy-start.2) | copy-done | bytes 6291480
  106.0 4.9 %copy.33 = f32[2,8,32,4096]{3,1,2,0:T(8,128)S(1)} copy(f32[2,8,32,4096]{3,2,1,0:T(8,128)S(1)} %bitcast.146) | data formatting | bytes 16777216
  110.9 6.6 %broadcast_multiply_fusion.1 = (f32[12,131072]{1,0:T(8,128)}, f32[12,131072]{1,0:T(8,128)}) fusion(f32[12,131072]{1,0:T(8,128)S(1)} %bitcast.143, f32[131072]{0:T(1024)S(1)} %bitcast.155, f32[131072]{0:T(1024)S(1)} %bitcast.154), kind=kLoop, calls=%fused_computation.17 | loop fusion | flops 3145728 | bytes 19922944 | tf_op jit(solution)/shard_map/mul | solution.py:90
  117.5 1.6 copy-done.3
  119.1 26.7 %fusion.2 = f32[37,37]{1,0:T(8,128)S(1)} fusion(f32[12,131072]{1,0:T(8,128)} %get-tuple-element.5, f32[12,131072]{1,0:T(8,128)} %get-tuple-element.4, f32[12,131072]{1,0:T(8,128)} %bitcast.144, f32[37]{0:T(128)S(1)} %pad.8.clone, f32[131072]{0:T(1024)S(1)} %bitcast.156), kind=kOutput, calls=%fused_computation.2 | convolution fusion | flops 2187198464 | bytes 19404280 | tf_op jit(solution)/shard_map/ip,jp->ij/dot_general | solution.py:92
  145.9 21.7 %fusion.17 = f32[37]{0:T(128)S(1)} fusion(f32[131072,1]{0,1:T(1,128)S(1)} %bitcast.158, f32[12,131072]{1,0:T(8,128)} %get-tuple-element.5, f32[12,131072]{1,0:T(8,128)} %get-tuple-element.4, f32[12,131072]{1,0:T(8,128)} %bitcast.145, f32[37]{0:T(128)S(1)} %pad.8.clone, f32[131072]{0:T(1024)S(1)} %bitcast.157), kind=kOutput, calls=%fused_computation.23 | convolution fusion | flops 77594624 | bytes 19923240 | tf_op jit(solution)/shard_map/ip,p->i/dot_general | solution.py:93
  167.5 41.4 %all-reduce.1 = (f32[37,37]{1,0:T(8,128)S(1)}, f32[37]{0:T(128)S(1)}) all-reduce(f32[37,37]{1,0:T(8,128)S(1)} %fusion.2, f32[37]{0:T(128)S(1)} %fusion.17), channel_id=1, replica_groups=mesh['det'=16,'strip'=8] {'strip'}, use_global_device_ids=true, to_apply=%region_0.1 | all-reduce | flops 1406 | bytes 11248 | tf_op jit(solution)/shard_map/psum | solution.py:94
  209.0 3.4 %cholesky.17 = f32[37,37]{1,0:T(8,128)S(1)} custom-call(f32[37,37]{1,0:T(8,128)S(1)} %fusion.43), custom_call_target="Cholesky" | custom-call | tf_op jit(solution)/shard_map/jit(cholesky)/cholesky | solution.py:96
  213.7 2.8 %custom-call.10 = f32[1,37,37]{1,2,0:T(8,128)S(1)} custom-call(f32[1,37,37]{2,1,0:T(8,128)S(1)} %fusion.39), custom_call_target="InvertDiagBlocksLowerTriangular" | custom-call | tf_op jit(solution)/shard_map/jit(_cho_solve)/triangular_solve | solution.py:97
  216.9 11.3 %fusion.12 = f32[1,32,4096]{2,0,1:T(1,128)S(1)} fusion(f32[12,32,4096]{2,1,0:T(8,128)} %copy-done.2, f32[37]{0:T(128)S(1)} %bitcast.159), kind=kOutput, calls=%fused_computation.14 | convolution fusion | flops 18874368 | bytes 6815892 | tf_op jit(solution)/shard_map/dot_general | solution.py:57
  228.3 11.4 %fusion.10 = f32[1,32,4096]{2,0,1:T(1,128)S(1)} fusion(f32[12,32,4096]{2,1,0:T(8,128)} %copy-done.2, f32[37]{0:T(128)S(1)} %bitcast.160), kind=kOutput, calls=%fused_computation.12 | convolution fusion | flops 18874368 | bytes 6815892 | tf_op jit(solution)/shard_map/dot_general | solution.py:58
  239.6 9.3 %fusion.8 = f32[1,32,4096]{2,0,1:T(1,128)S(1)} fusion(f32[12,32,4096]{2,1,0:T(8,128)S(1)} %bitcast.142, f32[37]{0:T(128)S(1)} %bitcast.161), kind=kOutput, calls=%fused_computation.10 | convolution fusion | flops 18874368 | bytes 6815892 | tf_op jit(solution)/shard_map/dot_general | solution.py:59
  249.5 2.5 %fusion.30 = f32[1,32,4096]{2,1,0:T(8,128)} fusion(f32[1,32,4096]{2,1,0:T(8,128)S(1)} %copy-done.4, f32[1,32,4096]{2,0,1:T(1,128)S(1)} %fusion.8, f32[1,32,4096]{2,0,1:T(1,128)S(1)} %fusion.10, f32[1,32,4096]{2,0,1:T(1,128)S(1)} %fusion.12, f32[]{:T(128)} %bitcast.44, f32[32]{0:T(128)S(1)} %multiply_add_fusion.1, f32[4096]{0:T(1024)S(1)} %multiply_add_fusion), kind=kLoop, calls=%fused_computation.41 | loop fusion | flops 786432 | bytes 2637956 | tf_op jit(solution)/shard_map/stack | solution.py:100
  (64 shorter events, 20.7 us)
Async XLA Ops:
  0.6 32.7 %copy-start = (f32[12,21]{1,0:T(8,128)S(1)}, f32[12,21]{1,0:T(8,128)}, u32[]{:S(2)}) copy-start(f32[12,21]{1,0:T(8,128)} %param.9) | copy-start | bytes 3028
  0.6 46.9 %copy-start.8 = (f32[12,21]{1,0:T(8,128)S(1)}, f32[12,21]{1,0:T(8,128)}, u32[]{:S(2)}) copy-start(f32[12,21]{1,0:T(8,128)} %param.8) | copy-start | bytes 3028
  22.7 16.8 %all-to-all-start = ((f32[16,1,32,256]{3,2,1,0:T(8,128)}), f32[16,1,32,256]{3,2,1,0:T(8,128)}, u32[]{:S(2)}, u32[]{:S(2)}) async-start(f32[16,1,32,256]{3,2,1,0:T(8,128)} %constant_dynamic-update-slice_fusion), calls=%async_computation | async-start | bytes 1048576 | tf_op jit(solution)/shard_map/all_to_all | solution.py:66
  40.6 15.9 %collective-permute-start = (f32[1,10,4096]{2,1,0:T(8,128)S(1)}, f32[1,10,4096]{2,1,0:T(8,128)S(1)}, u32[]{:S(2)}, u32[]{:S(2)}) collective-permute-start(f32[1,10,4096]{2,1,0:T(8,128)S(1)} %get-tuple-element.10), channel_id=1, source_target_pairs={{0,1},{1,2},{2,3},{3,4},{4,5},{5,6},{6,7},{8,9},{9,10},{10,11},{11... | collective-permute-start | bytes 491528 | tf_op jit(solution)/shard_map/ppermute | solution.py:21
  46.1 10.4 %collective-permute-start.1 = (f32[1,10,4096]{2,1,0:T(8,128)S(1)}, f32[1,10,4096]{2,1,0:T(8,128)S(1)}, u32[]{:S(2)}, u32[]{:S(2)}) collective-permute-start(f32[1,10,4096]{2,1,0:T(8,128)S(1)} %get-tuple-element.11), channel_id=1, source_target_pairs={{1,0},{2,1},{3,2},{4,3},{5,4},{6,5},{7,6},{9,8},{10,9},{11,10},{12... | collective-permute-start | bytes 491528 | tf_op jit(solution)/shard_map/ppermute | solution.py:24
  102.4 2.7 %copy-start.2 = (f32[12,32,4096]{2,1,0:T(8,128)}, f32[12,32,4096]{2,1,0:T(8,128)S(1)}, u32[]{:S(2)}) copy-start(f32[12,32,4096]{2,1,0:T(8,128)S(1)} %fusion.36) | copy-start | bytes 18874372
  110.9 8.3 %copy-start.3 = (f32[2,8,32,4096]{3,1,2,0:T(8,128)}, f32[2,8,32,4096]{3,1,2,0:T(8,128)S(1)}, u32[]{:S(2)}) copy-start(f32[2,8,32,4096]{3,1,2,0:T(8,128)S(1)} %copy.33) | copy-start | bytes 25165828
  110.9 8.3 %copy-start.5 = (f32[4,32,8,128]{3,1,2,0:T(8,128)S(1)}, f32[4,32,8,128]{3,1,2,0:T(8,128)}, u32[]{:S(2)}) copy-start(f32[4,32,8,128]{3,1,2,0:T(8,128)} %copy.36) | copy-start | bytes 1572868
  119.1 26.7 %copy-start.6 = (f32[1,1,32,4096]{3,1,2,0:T(1,128)S(1)}, f32[1,1,32,4096]{3,1,2,0:T(1,128)}, u32[]{:S(2)}) copy-start(f32[1,1,32,4096]{3,1,2,0:T(1,128)} %copy.37) | copy-start | bytes 1572868
  216.9 32.1 %copy-start.7 = (f32[1,37]{1,0:T(1,128)}, f32[1,37]{1,0:T(1,128)S(1)}, u32[]{:S(2)}) copy-start(f32[1,37]{1,0:T(1,128)S(1)} %fusion.40) | copy-start | bytes 448
  216.9 22.8 %slice-start = ((s8[6291456]{0:T(1024)(128)(4,1)}), s8[4194304]{0:T(1024)(128)(4,1)S(1)}, s32[]{:S(2)}) async-start(s8[6291456]{0:T(1024)(128)(4,1)} %bitcast.141), calls=%async_computation.1 | async-start | bytes 8388608
  216.9 35.2 %copy-start.1 = (f32[12,21]{1,0:T(8,128)S(1)}, f32[12,21]{1,0:T(8,128)}, u32[]{:S(2)}) copy-start(f32[12,21]{1,0:T(8,128)} %param.9) | copy-start | bytes 3028
  228.2 11.4 %slice-start.1 = ((s8[6291456]{0:T(1024)(128)(4,1)}), s8[2097152]{0:T(1024)(128)(4,1)S(1)}, s32[]{:S(2)}) async-start(s8[6291456]{0:T(1024)(128)(4,1)} %bitcast.141), calls=%async_computation.2 | async-start | bytes 4194304
  228.2 21.3 %copy-start.4 = (f32[1,32,4096]{2,1,0:T(8,128)S(1)}, f32[1,32,4096]{2,1,0:T(8,128)}, u32[]{:S(2)}) copy-start(f32[1,32,4096]{2,1,0:T(8,128)} %param.6) | copy-start | bytes 1572868
